TPU v7x, 32 devices: a whole 2x2x4 slice. The times are simulated.
32 devices in a mesh: rep: 16 (over z, y, core), shard: 2 (over x).
Axes of the slice: x: 2, y: 2, z: 4, core: 2. Of those that a mesh axis runs over, the one named last changes fastest.
Arguments:
- grads_query: bfloat16 [64, 960, 960], P(('rep', 'shard')), may hold values from -3000 to 3000
- master_query: float32 [960, 960], P('shard'), may hold values from -0.1875 to 0.1875
- moment_query: float32 [960, 960], P('shard'), may hold values from -6 to 6
- second_query: float32 [960, 960], P('shard'), may hold values from 0.25 to 4
- grads_keys: bfloat16 [64, 960, 320], P(('rep', 'shard')), may hold values from -3000 to 3000
- master_keys: float32 [960, 320], P('shard'), may hold values from -0.1875 to 0.1875
- moment_keys: float32 [960, 320], P('shard'), may hold values from -6 to 6
- second_keys: float32 [960, 320], P('shard'), may hold values from 0.25 to 4
Outputs:
- new_master_query: float32 [960, 960], P('shard')
- new_moment_query: float32 [960, 960], P('shard')
- new_second_query: float32 [960, 960], P('shard')
- weight_query: bfloat16 [960, 960], replicated
- new_master_keys: float32 [960, 320], P('shard')
- new_moment_keys: float32 [960, 320], P('shard')
- new_second_keys: float32 [960, 320], P('shard')
- weight_keys: bfloat16 [960, 320], replicated
All inputs are finite; a program needn't handle non-finite values.
Results may differ from a plain program's by a relative error of at most 0.001.
Values may be sent and summed in bfloat16 or wider, within the bound.
A program may use at most 128 MiB of HBM per device.

v0:
```python
import jax
import jax.numpy as jnp
from jax import lax
from jax.sharding import PartitionSpec as P

D = 960
KV = 320
STEP = 10


def adamw(grad_sum, master, moment, second, clip):
    grad = clip * grad_sum
    new_moment = 0.9 * moment + 0.1 * grad
    new_second = 0.999 * second + 0.001 * grad * grad
    mhat = new_moment / (1.0 - 0.9**STEP)
    vhat = new_second / (1.0 - 0.999**STEP)
    new_master = master - 0.02 * (mhat / (jnp.sqrt(vhat) + 1e-08) + 0.1 * master)
    return (new_master, new_moment, new_second, new_master.astype(jnp.bfloat16))


def local(
    grads_query,
    master_query,
    moment_query,
    second_query,
    grads_keys,
    master_keys,
    moment_keys,
    second_keys,
):
    local_query = jnp.sum(grads_query, axis=0, dtype=jnp.float32)
    local_keys = jnp.sum(grads_keys, axis=0, dtype=jnp.float32)
    rows_query, rows_keys = (
        lax.psum_scatter(
            local_query.astype(jnp.bfloat16), "shard", scatter_dimension=0, tiled=True
        ).astype(jnp.float32),
        lax.psum_scatter(
            local_keys.astype(jnp.bfloat16), "shard", scatter_dimension=0, tiled=True
        ).astype(jnp.float32),
    )
    sum_query, sum_keys = lax.psum((rows_query, rows_keys), "rep")
    partial_value = jnp.sum(sum_query * sum_query) + jnp.sum(sum_keys * sum_keys)
    total = lax.psum(partial_value, "shard")
    limit = jnp.sqrt(jnp.float32(D * D + D * KV))
    clip = jnp.minimum(jnp.float32(1.0), limit / (jnp.sqrt(total) + 1e-06))
    query_out = adamw(sum_query, master_query, moment_query, second_query, clip)
    keys_out = adamw(sum_keys, master_keys, moment_keys, second_keys, clip)
    weight_query, weight_keys = (
        lax.all_gather(query_out[3], "shard", axis=0, tiled=True),
        lax.all_gather(keys_out[3], "shard", axis=0, tiled=True),
    )
    return (
        query_out[0],
        query_out[1],
        query_out[2],
        weight_query,
        keys_out[0],
        keys_out[1],
        keys_out[2],
        weight_keys,
    )


def solution(mesh):
    in_specs = (
        P(("rep", "shard"), None, None),
        P("shard", None),
        P("shard", None),
        P("shard", None),
        P(("rep", "shard"), None, None),
        P("shard", None),
        P("shard", None),
        P("shard", None),
    )
    out_specs = (
        P("shard", None),
        P("shard", None),
        P("shard", None),
        P(),
        P("shard", None),
        P("shard", None),
        P("shard", None),
        P(),
    )
    return jax.shard_map(local, mesh=mesh, in_specs=in_specs, out_specs=out_specs, check_vma=False)
```

profile of v0, /device:TPU:1, one launch (start us, length us, event | category | flops | bytes accessed | tf_op | source)
XLA Modules:
  0.0 196.4 jit_solution(9995619279791070925)
XLA Ops:
  7.2 0.0 reduce-scatter.7.cloned.1.call-start
  7.2 1.7 reduce_sum.44
  8.9 1.2 copy.18
  10.0 0.0 reduce-scatter.7.cloned.1.call-update
  10.1 0.0 reduce-scatter.5.cloned.1.call-start
  10.1 4.9 %reduce_sum.42 = bf16[960,960]{1,0:T(8,128)(2,1)} reduce(bf16[2,960,960]{2,1,0:T(8,128)(2,1)} %param.8, bf16[]{:T(256)} %constant.15.clone.1), dimensions={0}, to_apply=%region_0.0 | reduce | flops 921600 | bytes 5529602 | tf_op jit(solution)/shard_map/reduce_sum | solution.py:31
  15.0 0.0 reduce-scatter.5.cloned.1.call-update
  15.1 0.0 all-gather.3.cloned.1.call-start
  15.1 14.7 %reduce-scatter.7.cloned.1.call-done = bf16[480,320]{1,0:T(8,128)(2,1)} async-done(((bf16[960,320]{1,0:T(8,128)(2,1)}), bf16[480,320]{1,0:T(8,128)(2,1)}) %reduce-scatter.7.cloned.1.call-update) | async-done | bytes 307216
  29.9 1.1 copy.19
  31.0 32.1 %reduce-scatter.5.cloned.1.call-done = bf16[480,960]{1,0:T(8,128)(2,1)} async-done(((bf16[960,960]{1,0:T(8,128)(2,1)}), bf16[480,960]{1,0:T(8,128)(2,1)}) %reduce-scatter.5.cloned.1.call-update) | async-done | bytes 921616 | tf_op jit(solution)/shard_map/reduce_scatter | solution.py:34
  63.1 72.9 %all-reduce.2 = (f32[480,960]{1,0:T(8,128)S(1)}, f32[480,320]{0,1:T(8,128)S(1)}) all-reduce(bf16[480,960]{1,0:T(8,128)(2,1)} %reduce-scatter.5.cloned.1.call-done, bf16[480,320]{0,1:T(8,128)(2,1)S(1)} %copy.19), channel_id=1, replica_groups=mesh['rep'=16,'shard'=2] {'rep'}, use_global_device_ids=true, to_apply=%region_2.0 | all-reduce | flops 614400 | bytes 3686400 | tf_op jit(solution)/shard_map/psum | solution.py:41
  136.0 1.1 multiply_reduce_fusion
  137.1 0.8 multiply_reduce_fusion.1
  139.2 4.3 %psum.23 = f32[]{:T(128)} all-reduce(f32[]{:T(128)S(6)} %add.46), channel_id=1, replica_groups=mesh['rep'=16,'shard'=2] {'shard'}, use_global_device_ids=true, to_apply=%region_8.0 | all-reduce | flops 1 | bytes 8 | tf_op jit(solution)/shard_map/psum | solution.py:43
  144.2 0.0 copy-start
  144.2 6.8 %fusion.3 = (bf16[480,960]{1,0:T(8,128)(2,1)}, f32[480,960]{1,0:T(8,128)}, f32[480,960]{1,0:T(8,128)}, f32[480,960]{1,0:T(8,128)}) fusion(f32[480,960]{1,0:T(8,128)} %param.9, f32[480,960]{1,0:T(8,128)S(1)} %get-tuple-element.8, f32[]{:T(128)S(6)} %min_shard_map.3, f32[480,960]{1,0:T(8,128)} %param.10, f32[480,960]{1,0:T(8,128)} %param.11), kind=kLoop, calls=%fused_computation.11 | loop fusion | flops 7833600 | bytes 13824004 | tf_op jit(solution)/shard_map/convert_element_type | solution.py:18
  151.1 0.0 all-gather.3.cloned.1.call-update
  151.1 0.0 copy-done
  151.1 2.9 %convert_bitcast_fusion = (bf16[1,480,320]{1,2,0:T(8,128)(2,1)S(1)}, f32[480,320]{0,1:T(8,128)}, f32[480,320]{0,1:T(8,128)}, f32[480,320]{0,1:T(8,128)}) fusion(f32[480,320]{0,1:T(8,128)S(1)} %copy-done, f32[480,320]{0,1:T(8,128)S(1)} %get-tuple-element.9, f32[]{:T(128)S(6)} %min_shard_map.3, f32[480,320]{0,1:T(8,128)} %param.14, f32[480,320]{0,1:T(8,128)} %param.15), kind=kLoop, calls=%fused_computation.10 | loop fusion | flops 2611200 | bytes 4608004
  154.0 6.6 %all-gather = bf16[2,480,320]{1,2,0:T(8,128)(2,1)S(1)} all-gather(bf16[1,480,320]{1,2,0:T(8,128)(2,1)S(1)} %get-tuple-element.10), channel_id=1, replica_groups=mesh['rep'=16,'shard'=2] {'shard'}, dimensions={0}, use_global_device_ids=true | all-gather | bytes 921600 | tf_op jit(solution)/shard_map/all_gather | solution.py:50
  160.6 0.7 copy.17
  161.3 1.5 reshape.17
  162.8 24.2 %all-gather.3.cloned.1.call-done = bf16[960,960]{1,0:T(8,128)(2,1)} async-done(((bf16[480,960]{1,0:T(8,128)(2,1)}), bf16[960,960]{1,0:T(8,128)(2,1)}) %all-gather.3.cloned.1.call-update) | async-done | bytes 1843216 | tf_op jit(solution)/shard_map/all_gather | solution.py:49
  186.9 3.0 %copy.25 = bf16[960,960]{1,0:T(8,128)(2,1)} copy(bf16[960,960]{1,0:T(8,128)(2,1)} %all-gather.3.cloned.1.call-done) | data formatting | bytes 3686400
Async XLA Ops:
  7.2 22.7 %reduce-scatter.7.cloned.1.call-start = ((), (), s32[]{:S(2)}) async-start(), calls=%async_computation.4 | async-start | bytes 1105920
  10.1 53.0 %reduce-scatter.5.cloned.1.call-start = ((), (), s32[]{:S(2)}) async-start(), calls=%async_computation.2 | async-start | bytes 2949120 | tf_op jit(solution)/shard_map/reduce_scatter | solution.py:34
  15.1 171.8 %all-gather.3.cloned.1.call-start = ((), (), s32[]{:S(2)}) async-start(), calls=%async_computation.3 | async-start | bytes 2949120 | tf_op jit(solution)/shard_map/all_gather | solution.py:49
  144.2 6.9 %copy-start = (f32[480,320]{0,1:T(8,128)S(1)}, f32[480,320]{0,1:T(8,128)}, u32[]{:S(2)}) copy-start(f32[480,320]{0,1:T(8,128)} %param.13) | copy-start | bytes 1843204
Sparse Core Ops, SparseCore 0:
  10.8 18.9 reduce-scatter.6
  32.7 30.3 reduce-scatter.4
  151.2 35.6 all-gather.2
where the time goes:
time: 197 us; the launch traced here: 196 us
  blocking collectives  83.8 us (43%)
  waiting for transfers between devices  71 us (36%)
  other arithmetic  18.2 us (9%)
  between operations  15.8 us (8%)
  local copies, waits for them, and re-layouts  7.4 us (4%)
    psum x1, blocking collectives, local(): sum_query, sum_keys = lax.psum((rows_query, rows_keys), 'rep')  72.9 us
    reduce_scatter x1, waiting for transfers between devices, local(): lax.psum_scatter(local_query.astype(jnp.bfloat16), 'shard', scatter_dimen...  32.1 us
    all_gather x1, waiting for transfers between devices, local(): lax.all_gather(query_out[3], 'shard', axis=0, tiled=True)  24.2 us
    unnamed x4, waiting for transfers between devices  14.8 us
    convert_element_type x1, other arithmetic, adamw(): return (new_master, new_moment, new_second, new_master.astype(jnp.bfloat16))  6.82 us
    unnamed x6, local copies, waits for them, and re-layouts  6.73 us
    all_gather x1, blocking collectives, local(): lax.all_gather(keys_out[3], 'shard', axis=0, tiled=True)  6.59 us
    reduce_sum x1, other arithmetic, local(): local_query = jnp.sum(grads_query, axis=0, dtype=jnp.float32)  4.94 us
  transfers between devices with their start and end apart: 3, of which 3 were waited for; matrix products, arithmetic and copies ran while one was open for 6% of the time, Pallas kernels for 0%

commit v1 on v0

v1 whole, which is shorter than its diff:
```python
import functools

import jax
import jax.numpy as jnp
from jax import lax
from jax.experimental import pallas as pl
from jax.experimental.pallas import tpu as pltpu
from jax.sharding import PartitionSpec as P

D = 960
KV = 320
STEP = 10
CORES = 2
RT = 16
WIDE = D + KV
MAIN = KV // 128 * 128
MESH = pl.DeviceIdType.MESH
F32 = jnp.float32
BF16 = jnp.bfloat16


def join(q, k):
    return jnp.concatenate([q, k[:, MAIN:], k[:, :MAIN]], axis=1)


def split(wide):
    rest = KV - MAIN
    return wide[:, :D], jnp.concatenate([wide[:, D + rest :], wide[:, D : D + rest]], axis=1)


def adamw(grad_sum, master, moment, second, clip):
    grad = clip * grad_sum
    new_moment = 0.9 * moment + 0.1 * grad
    new_second = 0.999 * second + 0.001 * grad * grad
    mhat = new_moment / (1.0 - 0.9**STEP)
    vhat = new_second / (1.0 - 0.999**STEP)
    new_master = master - 0.02 * (mhat / (jnp.sqrt(vhat) + 1e-08) + 0.1 * master)
    return new_master, new_moment, new_second


def kernel(
    zy_n, np_n, pr, rpc,
    gq_hbm, mq_hbm, oq_hbm, sq_hbm, gk_hbm, mk_hbm, ok_hbm, sk_hbm,
    nmq_hbm, noq_hbm, nsq_hbm, nmk_hbm, nok_hbm, nsk_hbm, w_hbm,
    gq, gk, mq, oq, sq, mk, ok, sk,
    cs, cr, xs, xr, zs, zr, own, g, w, norm, normx,
    in_sem, st_sem, out_sem, w_sem,
    cs_s, cr_s, xs_s, xr_s, zs_s, zr_s,
    ags_s, agr_s, fs_s, fr_s, ws_s, wr_s, vs_s, vr_s, ns_s, nr_s,
):
    rep = lax.axis_index("rep")
    x = lax.axis_index("shard")
    c = lax.rem(rep, CORES)
    zy = lax.div(rep, CORES)
    half = CORES * rpc
    core_dev = (zy * CORES + 1 - c, x)
    x_dev = (rep, 1 - x)
    tiles = pr // RT

    def peer(j):
        return lax.rem(zy + j, zy_n)

    def zy_dev(q):
        return (q * CORES + c, x)

    def piece(k):
        return lax.rem(zy + 1 + k, np_n)

    def rcopy(src, dst, s, r, dev):
        return pltpu.make_async_remote_copy(
            src_ref=src, dst_ref=dst, send_sem=s, recv_sem=r, device_id=dev, device_id_type=MESH
        )

    grads_in = [
        pltpu.make_async_copy(gq_hbm, gq, in_sem.at[0]),
        pltpu.make_async_copy(gk_hbm, gk, in_sem.at[1]),
    ]
    for one in grads_in:
        one.start()
    states = [(mq_hbm, mq), (oq_hbm, oq), (sq_hbm, sq), (mk_hbm, mk), (ok_hbm, ok), (sk_hbm, sk)]
    states_in = [
        pltpu.make_async_copy(src, dst, st_sem.at[i]) for i, (src, dst) in enumerate(states)
    ]
    for one in states_in:
        one.start()

    barrier = pltpu.get_barrier_semaphore()
    pl.semaphore_signal(barrier, inc=1, device_id=core_dev, device_id_type=MESH)
    pl.semaphore_signal(barrier, inc=1, device_id=x_dev, device_id_type=MESH)

    @pl.loop(1, zy_n)
    def _(j):
        pl.semaphore_signal(barrier, inc=1, device_id=zy_dev(peer(j)), device_id_type=MESH)

    for one in grads_in:
        one.wait()
    pl.semaphore_wait(barrier, zy_n + 1)

    def rows_of(p, t):
        return jnp.minimum(p * pr + t * RT, rpc - RT)

    def lsum(xh, core, p, t):
        row = pl.ds(pl.multiple_of(xh * half + core * rpc + rows_of(p, t), RT), RT)
        q = gq[0, row, :].astype(F32)
        k = gk[0, row, :].astype(F32)
        for m in range(1, gq.shape[0]):
            q = q + gq[m, row, :].astype(F32)
            k = k + gk[m, row, :].astype(F32)
        return join(q, k)

    def tile(t):
        return pl.ds(t * RT, RT)

    def core_copy(k):
        return rcopy(cs.at[k], cr.at[k], cs_s.at[k], cr_s.at[k], core_dev)

    def x_copy(k):
        return rcopy(xs.at[k], xr.at[k], xs_s.at[k], xr_s.at[k], x_dev)

    def zy_copy(k):
        return rcopy(zs.at[k], zr.at[zy], zs_s.at[k], zr_s.at[zy], zy_dev(piece(k)))

    def zy_arrival(s):
        return rcopy(zs.at[0], zr.at[s], zs_s.at[0], zr_s.at[s], zy_dev(s))

    @pl.loop(0, np_n)
    def _(k):
        p = piece(k)
        for xh in range(2):
            for t in range(tiles):
                cs[k, xh, tile(t), :] = lsum(xh, 1 - c, p, t).astype(BF16)
        core_copy(k).start()

    @pl.loop(0, np_n)
    def _(k):
        p = piece(k)
        core_copy(k).wait_recv()
        for t in range(tiles):
            part = lsum(1 - x, c, p, t) + cr[k, 1 - x, tile(t), :].astype(F32)
            xs[k, tile(t), :] = part.astype(BF16)
        x_copy(k).start()

    @pl.loop(0, np_n)
    def _(k):
        p = piece(k)
        x_copy(k).wait_recv()
        for t in range(tiles):
            part = lsum(x, c, p, t) + cr[k, x, tile(t), :].astype(F32)
            part = part + xr[k, tile(t), :].astype(F32)

            @pl.when(p == zy)
            def _():
                own[tile(t), :] = part

            @pl.when(p != zy)
            def _():
                zs[k, tile(t), :] = part.astype(BF16)

        @pl.when(p != zy)
        def _():
            zy_copy(k).start()

    def norm_copy(i, dev):
        return rcopy(norm.at[i], normx.at[i], ns_s.at[i], nr_s.at[i], dev)

    def fold(a):
        total = jnp.zeros((8, 128), F32)
        for r in range(0, a.shape[0], 8):
            for l in range(0, a.shape[1], 128):
                total = total + a[r : r + 8, l : l + 128]
        return total

    def gather_copy(j):
        return rcopy(g.at[c, zy], g.at[c, zy], ags_s.at[j], agr_s.at[zy], zy_dev(peer(j)))

    def gather_arrival(p):
        return rcopy(g.at[c, p], g.at[c, p], ags_s.at[0], agr_s.at[p], zy_dev(p))

    def forward(core, p):
        return rcopy(g.at[core, p], g.at[core, p], fs_s.at[p], fr_s.at[p], core_dev)

    norm[0] = jnp.zeros((8, 128), F32)

    @pl.when(zy < np_n)
    def _():
        @pl.loop(1, zy_n)
        def _(j):
            zy_arrival(lax.rem(zy + zy_n - j, zy_n)).wait_recv()

        total = jnp.zeros((8, 128), F32)
        for t in range(tiles):

            def add(j, acc):
                return acc + zr[peer(j), tile(t), :].astype(F32)

            acc = lax.fori_loop(1, zy_n, add, own[tile(t), :])
            g[c, zy, tile(t), :] = acc.astype(BF16)
            valid = (zy * pr + t * RT < rpc).astype(F32)
            total = total + fold(acc * acc) * valid
        norm[0] = total

    norm_copy(0, core_dev).start()

    @pl.when(zy < np_n)
    def _():
        forward(c, zy).start()

        @pl.loop(1, zy_n)
        def _(j):
            gather_copy(j).start()

    norm_copy(0, core_dev).wait_recv()
    norm[1] = norm[0] + normx[0]
    norm_copy(1, x_dev).start()
    norm_copy(1, x_dev).wait_recv()
    norm[2] = norm[1] + normx[1]

    def norm_out(j):
        return rcopy(norm.at[2], normx.at[2 + zy], ns_s.at[2 + j], nr_s.at[2 + zy], zy_dev(peer(j)))

    def norm_in(s):
        return rcopy(norm.at[2], normx.at[2 + s], ns_s.at[2], nr_s.at[2 + s], zy_dev(s))

    @pl.loop(1, zy_n)
    def _(j):
        norm_out(j).start()

    normx[2 + zy] = norm[2]

    @pl.loop(1, zy_n)
    def _(j):
        norm_in(peer(j)).wait_recv()

    total = lax.fori_loop(0, zy_n, lambda s, acc: acc + normx[2 + s], jnp.zeros((8, 128), F32))
    total = jnp.sum(jnp.sum(total, axis=1, keepdims=True), axis=0, keepdims=True)
    limit = jnp.sqrt(jnp.full((1, 1), D * D + D * KV, F32))
    clip = jnp.minimum(1.0, limit / (jnp.sqrt(total) + 1e-06))

    for one in states_in:
        one.wait()

    def weights_over(p):
        return rcopy(w.at[x, c, p], w.at[x, c, p], ws_s.at[p], wr_s.at[p], x_dev)

    def weights_in(p):
        return rcopy(w.at[1 - x, c, p], w.at[1 - x, c, p], ws_s.at[p], wr_s.at[p], x_dev)

    def weights_forward(p):
        return rcopy(w.at[1 - x, c, p], w.at[1 - x, c, p], vs_s.at[p], vr_s.at[p], core_dev)

    def weights_last(p):
        return rcopy(w.at[1 - x, 1 - c, p], w.at[1 - x, 1 - c, p], vs_s.at[p], vr_s.at[p], core_dev)

    def update(core, p):
        for t in range(tiles):
            row = pl.ds(pl.multiple_of(core * rpc + rows_of(p, t), RT), RT)

            @pl.when(p * pr + t * RT < rpc)
            def _():
                gsq, gsk = split(g[core, p, tile(t), :].astype(F32))
                m, o, s = adamw(gsq, mq[row, :], oq[row, :], sq[row, :], clip)
                mq[row, :] = m
                oq[row, :] = o
                sq[row, :] = s
                km, ko, ks = adamw(gsk, mk[row, :], ok[row, :], sk[row, :], clip)
                mk[row, :] = km
                ok[row, :] = ko
                sk[row, :] = ks
                w[x, core, p, tile(t), :] = join(m, km).astype(BF16)

    outs = [(mq, nmq_hbm), (oq, noq_hbm), (sq, nsq_hbm), (mk, nmk_hbm), (ok, nok_hbm), (sk, nsk_hbm)]

    def out_copies(core, n):
        row = pl.ds(pl.multiple_of(core * rpc, RT), rpc)
        return [
            pltpu.make_async_copy(src.at[row, :], dst.at[row, :], out_sem.at[n, i])
            for i, (src, dst) in enumerate(outs)
        ]

    @pl.loop(0, np_n)
    def _(k):
        p = lax.rem(zy + np_n - k, np_n)

        @pl.when(p != zy)
        def _():
            gather_arrival(p).wait_recv()
            forward(c, p).start()

        update(c, p)
        weights_over(p).start()

    mine_out = out_copies(c, 0)
    for one in mine_out:
        one.start()

    @pl.loop(0, np_n)
    def _(k):
        p = lax.rem(zy + np_n - k, np_n)
        forward(1 - c, p).wait_recv()
        update(1 - c, p)

    other_out = out_copies(1 - c, 1)
    for one in other_out:
        one.start()
    w_own = pltpu.make_async_copy(w.at[x], w_hbm.at[x], w_sem.at[0])
    w_own.start()

    @pl.loop(0, np_n)
    def _(k):
        p = lax.rem(zy + np_n - k, np_n)
        weights_in(p).wait_recv()
        weights_forward(p).start()

    w_c = pltpu.make_async_copy(w.at[1 - x, c], w_hbm.at[1 - x, c], w_sem.at[1])
    w_c.start()

    @pl.loop(0, np_n)
    def _(k):
        weights_last(lax.rem(zy + np_n - k, np_n)).wait_recv()

    w_o = pltpu.make_async_copy(w.at[1 - x, 1 - c], w_hbm.at[1 - x, 1 - c], w_sem.at[2])
    w_o.start()

    @pl.loop(0, np_n)
    def _(k):
        core_copy(k).wait_send()
        x_copy(k).wait_send()

        @pl.when(piece(k) != zy)
        def _():
            zy_copy(k).wait_send()

        forward(c, k).wait_send()
        weights_over(k).wait_send()
        weights_forward(k).wait_send()

    @pl.when(zy < np_n)
    def _():
        @pl.loop(1, zy_n)
        def _(j):
            gather_copy(j).wait_send()

    @pl.loop(1, zy_n)
    def _(j):
        norm_out(j).wait_send()

    norm_copy(0, core_dev).wait_send()
    norm_copy(1, x_dev).wait_send()
    for one in mine_out + other_out + [w_own, w_c, w_o]:
        one.wait()


def local(zy_n, grads_query, master_query, moment_query, second_query, grads_keys, master_keys, moment_keys, second_keys):
    half = master_query.shape[0]
    rpc = half // CORES
    tiles_all = rpc // RT
    per = -(-tiles_all // zy_n)
    np_n = -(-tiles_all // per)
    pr = per * RT
    states = [master_query, moment_query, second_query, master_keys, moment_keys, second_keys]
    sem = lambda n: pltpu.SemaphoreType.DMA((n,))
    any_spec = pl.BlockSpec(memory_space=pl.ANY)
    outs = pl.pallas_call(
        functools.partial(kernel, zy_n, np_n, pr, rpc),
        out_shape=[jax.ShapeDtypeStruct(a.shape, F32) for a in states]
        + [jax.ShapeDtypeStruct((2, CORES, np_n, pr, WIDE), BF16)],
        in_specs=[any_spec] * 8,
        out_specs=[any_spec] * 7,
        scratch_shapes=[
            pltpu.VMEM(grads_query.shape, BF16),
            pltpu.VMEM(grads_keys.shape, BF16),
        ]
        + [pltpu.VMEM(a.shape, F32) for a in states]
        + [
            pltpu.VMEM((np_n, 2, pr, WIDE), BF16),
            pltpu.VMEM((np_n, 2, pr, WIDE), BF16),
            pltpu.VMEM((np_n, pr, WIDE), BF16),
            pltpu.VMEM((np_n, pr, WIDE), BF16),
            pltpu.VMEM((np_n, pr, WIDE), BF16),
            pltpu.VMEM((zy_n, pr, WIDE), BF16),
            pltpu.VMEM((pr, WIDE), F32),
            pltpu.VMEM((CORES, np_n, pr, WIDE), BF16),
            pltpu.VMEM((2, CORES, np_n, pr, WIDE), BF16),
            pltpu.VMEM((3, 8, 128), F32),
            pltpu.VMEM((2 + zy_n, 8, 128), F32),
            sem(2), sem(6), pltpu.SemaphoreType.DMA((2, 6)), sem(3),
            sem(np_n), sem(np_n), sem(np_n), sem(np_n), sem(np_n), sem(zy_n),
            sem(zy_n), sem(np_n), sem(np_n), sem(np_n),
            sem(np_n), sem(np_n), sem(np_n), sem(np_n), sem(2 + zy_n), sem(2 + zy_n),
        ],
        compiler_params=pltpu.CompilerParams(
            collective_id=0, has_side_effects=True, vmem_limit_bytes=56 << 20
        ),
    )(grads_query, master_query, moment_query, second_query, grads_keys, master_keys, moment_keys, second_keys)
    weights = outs[6].reshape(2, CORES, np_n * pr, WIDE)[:, :, :rpc, :].reshape(2 * half, WIDE)
    weight_query, weight_keys = split(weights)
    return (*outs[0:3], weight_query, *outs[3:6], weight_keys)


def solution(mesh):
    zy_n = mesh.shape["rep"] // CORES
    rows = P("shard", None)
    grads = P(("rep", "shard"), None, None)
    in_specs = (grads, rows, rows, rows, grads, rows, rows, rows)
    out_specs = (rows, rows, rows, P(), rows, rows, rows, P())
    return jax.shard_map(
        functools.partial(local, zy_n), mesh=mesh, in_specs=in_specs, out_specs=out_specs, check_vma=False
    )
```

time: 197 us -> 89.1 us (0.45)
  blocking collectives: 83.8 us -> 0 us
  waiting for transfers between devices: 71 us -> 0 us
  Pallas kernels: 0 us -> 65.7 us
  other arithmetic: 18.2 us -> 0.07 us
  between operations: 15.8 us -> 0.71 us
  local copies, waits for them, and re-layouts: 7.4 us -> 22.2 us
    psum x2 -> x0, blocking collectives: 77.2 us -> none  [the longest x1 72.9 us: local(): sum_query, sum_keys = lax.psum((rows_query, rows_keys), 'rep')]
    pallas_call x0 -> x1, Pallas kernels: none -> 65.7 us  [local(): pl.pallas_call(functools.partial(kernel, zy_n, np_n, pr, rpc), out_shape=...]
    reduce_scatter x1 -> x0, waiting for transfers between devices: 32.1 us -> none  [local(): lax.psum_scatter(local_query.astype(jnp.bfloat16), 'shard', scatter_dimen...]
    all_gather x1 -> x0, waiting for transfers between devices: 24.2 us -> none  [local(): lax.all_gather(query_out[3], 'shard', axis=0, tiled=True)]
    unnamed x4 -> x0, waiting for transfers between devices: 14.8 us -> none
    unnamed x6 -> x25, local copies, waits for them, and re-layouts: 6.73 us -> 20.4 us
    reduce_sum x4 -> x0, other arithmetic: 8.47 us -> none  [the longest x1 4.94 us: local(): local_query = jnp.sum(grads_query, axis=0, dtype=jnp.float32)]
    convert_element_type x1 -> x0, other arithmetic: 6.82 us -> none  [adamw(): return (new_master, new_moment, new_second, new_master.astype(jnp.bfloat16))]
  transfers between devices with their start and end apart: 3 -> 0, of which waited for: 3 -> 0; matrix products, arithmetic and copies ran while one was open for 6% -> 0% of each run, Pallas kernels for 0% -> 0%
where the time goes in v1:
time: 89.1 us; the launch traced here: 88.7 us
  Pallas kernels  65.7 us (74%)
  local copies, waits for them, and re-layouts  22.2 us (25%)
    pallas_call x1, Pallas kernels, local(): pl.pallas_call(functools.partial(kernel, zy_n, np_n, pr, rpc), out_shape=...  65.7 us
    unnamed x25, local copies, waits for them, and re-layouts  20.4 us

profile of v1, /device:TPU:1, one launch (start us, length us, event | category | flops | bytes accessed | tf_op | source)
XLA Modules:
  0.0 88.7 jit_solution(6575760091489488608)
XLA Ops:
  0.6 0.0 copy-start.6
  0.6 0.0 copy-start.4
  0.7 2.4 %copy.26.mk_hbm = f32[480,320]{1,0:T(8,128)} copy(f32[480,320]{0,1:T(8,128)} %param.13) | data formatting | bytes 1228800 | tf_op args[5]
  3.0 2.2 %copy.27.ok_hbm = f32[480,320]{1,0:T(8,128)} copy(f32[480,320]{0,1:T(8,128)} %param.14) | data formatting | bytes 1228800 | tf_op args[6]
  5.2 0.0 copy-done.6
  5.2 1.1 %copy.28.sk_hbm = f32[480,320]{1,0:T(8,128)} copy(f32[480,320]{0,1:T(8,128)S(1)} %copy-done.6) | data formatting | bytes 1228800 | tf_op args[7]
  6.3 0.0 copy-done.4
  6.3 1.6 %copy.25.gk_hbm = bf16[2,960,320]{2,1,0:T(8,128)(2,1)} copy(bf16[2,960,320]{1,2,0:T(8,128)(2,1)S(1)} %copy-done.4) | data formatting | bytes 2457600 | tf_op args[4]
  7.9 65.7 %shard_map.143 = (f32[480,960]{1,0:T(8,128)}, f32[480,960]{1,0:T(8,128)}, f32[480,960]{1,0:T(8,128)}, f32[480,320]{1,0:T(8,128)}, f32[480,320]{1,0:T(8,128)}, /*...) custom-call(bf16[2,960,960]{2,1,0:T(8,128)(2,1)} %gq_hbm.1, f32[480,960]{1,0:T(8,128)} %mq_hbm.1, ...), custom_call_target="tpu_custom_call" | custom-call | tf_op jit(solution)/shard_map/pallas_call | solution.py:363
  73.6 0.0 copy-start.5
  73.6 0.0 copy-start
  73.6 2.4 %copy.29 = f32[480,320]{0,1:T(8,128)} copy(f32[480,320]{1,0:T(8,128)} %get-tuple-element.34) | data formatting | bytes 1228800
  76.0 2.2 %copy.30 = f32[480,320]{0,1:T(8,128)} copy(f32[480,320]{1,0:T(8,128)} %get-tuple-element.35) | data formatting | bytes 1228800
  78.2 0.0 copy-done.5
  78.2 1.1 %copy.31 = f32[480,320]{0,1:T(8,128)} copy(f32[480,320]{1,0:T(8,128)S(1)} %copy-done.5) | data formatting | bytes 1228800
  79.3 0.0 copy-done
  79.3 0.2 slice.16
  79.4 0.1 slice.19
  79.6 1.5 %slice.17 = bf16[960,960]{1,0:T(8,128)(2,1)} slice(bf16[960,1280]{1,0:T(8,128)(2,1)S(1)} %bitcast.4), slice={[0:960], [0:960]} | slice | bytes 3686400 | tf_op jit(solution)/shard_map/slice | solution.py:28
  81.2 0.0 copy-start.3
  81.2 0.1 pad_maximum_fusion
  81.2 1.1 %copy.32 = bf16[960,320]{0,1:T(8,128)(2,1)} copy(bf16[960,320]{1,0:T(8,128)(2,1)S(1)} %pad_maximum_fusion) | data formatting | bytes 1228800
  82.3 0.6 copy-done.3
  82.9 0.0 copy-start.2
  82.9 1.3 %copy.36 = f32[480,960]{1,0:T(8,128)} copy(f32[480,960]{1,0:T(8,128)S(1)} %copy-done.3) | data formatting | bytes 3686400
  84.2 1.0 %copy-done.2 = f32[480,960]{1,0:T(8,128)S(1)} copy-done((f32[480,960]{1,0:T(8,128)S(1)}, f32[480,960]{1,0:T(8,128)}, u32[]{:S(2)}) %copy-start.2) | copy-done | bytes 1843224
  85.2 0.0 copy-start.1
  85.2 1.3 %copy.37 = f32[480,960]{1,0:T(8,128)} copy(f32[480,960]{1,0:T(8,128)S(1)} %copy-done.2) | data formatting | bytes 3686400
  86.5 1.0 %copy-done.1 = f32[480,960]{1,0:T(8,128)S(1)} copy-done((f32[480,960]{1,0:T(8,128)S(1)}, f32[480,960]{1,0:T(8,128)}, u32[]{:S(2)}) %copy-start.1) | copy-done | bytes 1843224
  87.5 1.3 %copy.38 = f32[480,960]{1,0:T(8,128)} copy(f32[480,960]{1,0:T(8,128)S(1)} %copy-done.1) | data formatting | bytes 3686400
  (1 shorter events, 0.0 us)
Async XLA Ops:
  0.6 4.6 %copy-start.6 = (f32[480,320]{0,1:T(8,128)S(1)}, f32[480,320]{0,1:T(8,128)}, u32[]{:S(2)}) copy-start(f32[480,320]{0,1:T(8,128)} %param.15) | copy-start | bytes 1843204
  0.6 5.7 %copy-start.4 = (bf16[2,960,320]{1,2,0:T(8,128)(2,1)S(1)}, bf16[2,960,320]{1,2,0:T(8,128)(2,1)}, u32[]{:S(2)}) copy-start(bf16[2,960,320]{1,2,0:T(8,128)(2,1)} %param.12) | copy-start | bytes 3686404
  73.6 4.6 %copy-start.5 = (f32[480,320]{1,0:T(8,128)S(1)}, f32[480,320]{1,0:T(8,128)}, u32[]{:S(2)}) copy-start(f32[480,320]{1,0:T(8,128)} %get-tuple-element.36) | copy-start | bytes 1843204
  73.6 5.7 %copy-start = (bf16[2,2,8,32,1280]{4,3,2,1,0:T(8,128)(2,1)S(1)}, bf16[2,2,8,32,1280]{4,3,2,1,0:T(8,128)(2,1)}, u32[]{:S(2)}) copy-start(bf16[2,2,8,32,1280]{4,3,2,1,0:T(8,128)(2,1)} %get-tuple-element.18) | copy-start | bytes 7864324
  81.2 1.8 %copy-start.3 = (f32[480,960]{1,0:T(8,128)S(1)}, f32[480,960]{1,0:T(8,128)}, u32[]{:S(2)}) copy-start(f32[480,960]{1,0:T(8,128)} %get-tuple-element.46) | copy-start | bytes 5529604
  82.9 2.3 %copy-start.2 = (f32[480,960]{1,0:T(8,128)S(1)}, f32[480,960]{1,0:T(8,128)}, u32[]{:S(2)}) copy-start(f32[480,960]{1,0:T(8,128)} %get-tuple-element.47) | copy-start | bytes 5529604
  85.2 2.3 %copy-start.1 = (f32[480,960]{1,0:T(8,128)S(1)}, f32[480,960]{1,0:T(8,128)}, u32[]{:S(2)}) copy-start(f32[480,960]{1,0:T(8,128)} %get-tuple-element.48) | copy-start | bytes 5529604

commit v2 on v1

--- a/solution.py
+++ b/solution.py
@@ -42,11 +42,11 @@
     zy_n, np_n, pr, rpc,
     gq_hbm, mq_hbm, oq_hbm, sq_hbm, gk_hbm, mk_hbm, ok_hbm, sk_hbm,
     nmq_hbm, noq_hbm, nsq_hbm, nmk_hbm, nok_hbm, nsk_hbm, w_hbm,
-    gq, gk, mq, oq, sq, mk, ok, sk,
+    gq, gk, mq, oq, sq, mkt, okt, skt, mk, ok, sk, lk,
     cs, cr, xs, xr, zs, zr, own, g, w, norm, normx,
     in_sem, st_sem, out_sem, w_sem,
     cs_s, cr_s, xs_s, xr_s, zs_s, zr_s,
-    ags_s, agr_s, fs_s, fr_s, ws_s, wr_s, vs_s, vr_s, ns_s, nr_s,
+    ags_s, agr_s, is_s, fs_s, fr_s, ws_s, wr_s, vs_s, vr_s, ns_s, nr_s,
 ):
     rep = lax.axis_index("rep")
     x = lax.axis_index("shard")
@@ -71,18 +71,28 @@
             src_ref=src, dst_ref=dst, send_sem=s, recv_sem=r, device_id=dev, device_id_type=MESH
         )
 
+    inner = lax.rem(zy, 2)
+    outer = lax.div(zy, 2)
+    outer_n = zy_n // 2
+
+    def grads_copy(i, xh, core):
+        row = pl.ds(pl.multiple_of(xh * half + core * rpc, RT), rpc)
+        return pltpu.make_async_copy(gq_hbm.at[:, row, :], gq.at[:, row, :], in_sem.at[i])
+
+    keys_in = pltpu.make_async_copy(gk_hbm, gk, in_sem.at[4])
     grads_in = [
-        pltpu.make_async_copy(gq_hbm, gq, in_sem.at[0]),
-        pltpu.make_async_copy(gk_hbm, gk, in_sem.at[1]),
+        grads_copy(0, 0, 1 - c),
+        grads_copy(1, 1, 1 - c),
+        grads_copy(2, 1 - x, c),
+        grads_copy(3, x, c),
     ]
+    keys_in.start()
     for one in grads_in:
         one.start()
-    states = [(mq_hbm, mq), (oq_hbm, oq), (sq_hbm, sq), (mk_hbm, mk), (ok_hbm, ok), (sk_hbm, sk)]
+    states = [(mq_hbm, mq), (oq_hbm, oq), (sq_hbm, sq), (mk_hbm, mkt), (ok_hbm, okt), (sk_hbm, skt)]
     states_in = [
         pltpu.make_async_copy(src, dst, st_sem.at[i]) for i, (src, dst) in enumerate(states)
     ]
-    for one in states_in:
-        one.start()
 
     barrier = pltpu.get_barrier_semaphore()
     pl.semaphore_signal(barrier, inc=1, device_id=core_dev, device_id_type=MESH)
@@ -92,8 +102,15 @@
     def _(j):
         pl.semaphore_signal(barrier, inc=1, device_id=zy_dev(peer(j)), device_id_type=MESH)
 
-    for one in grads_in:
-        one.wait()
+    keys_in.wait()
+    for lane in range(0, gk.shape[2], 128):
+        lanes = slice(lane, min(lane + 128, gk.shape[2]))
+        k = gk[0, :, lanes].astype(F32)
+        for m in range(1, gk.shape[0]):
+            k = k + gk[m, :, lanes].astype(F32)
+        lk[lanes, :] = k.T
+    grads_in[0].wait()
+    grads_in[1].wait()
     pl.semaphore_wait(barrier, zy_n + 1)
 
     def rows_of(p, t):
@@ -102,11 +119,9 @@
     def lsum(xh, core, p, t):
         row = pl.ds(pl.multiple_of(xh * half + core * rpc + rows_of(p, t), RT), RT)
         q = gq[0, row, :].astype(F32)
-        k = gk[0, row, :].astype(F32)
         for m in range(1, gq.shape[0]):
             q = q + gq[m, row, :].astype(F32)
-            k = k + gk[m, row, :].astype(F32)
-        return join(q, k)
+        return join(q, lk[row, :])
 
     def tile(t):
         return pl.ds(t * RT, RT)
@@ -130,6 +145,11 @@
             for t in range(tiles):
                 cs[k, xh, tile(t), :] = lsum(xh, 1 - c, p, t).astype(BF16)
         core_copy(k).start()
+
+    for one in states_in:
+        one.start()
+    grads_in[2].wait()
+    grads_in[3].wait()
 
     @pl.loop(0, np_n)
     def _(k):
@@ -140,6 +160,10 @@
             xs[k, tile(t), :] = part.astype(BF16)
         x_copy(k).start()
 
+    for i, (src, dst) in enumerate([(mkt, mk), (okt, ok), (skt, sk)]):
+        states_in[3 + i].wait()
+        dst[...] = src[...].T
+
     @pl.loop(0, np_n)
     def _(k):
         p = piece(k)
@@ -159,9 +183,6 @@
         @pl.when(p != zy)
         def _():
             zy_copy(k).start()
-
-    def norm_copy(i, dev):
-        return rcopy(norm.at[i], normx.at[i], ns_s.at[i], nr_s.at[i], dev)
 
     def fold(a):
         total = jnp.zeros((8, 128), F32)
@@ -171,7 +192,11 @@
         return total
 
     def gather_copy(j):
-        return rcopy(g.at[c, zy], g.at[c, zy], ags_s.at[j], agr_s.at[zy], zy_dev(peer(j)))
+        to = lax.rem(outer + j, outer_n) * 2 + inner
+        return rcopy(g.at[c, zy], g.at[c, zy], ags_s.at[j], agr_s.at[zy], zy_dev(to))
+
+    def inner_copy(p):
+        return rcopy(g.at[c, p], g.at[c, p], is_s.at[p], agr_s.at[p], zy_dev(zy + 1 - 2 * inner))
 
     def gather_arrival(p):
         return rcopy(g.at[c, p], g.at[c, p], ags_s.at[0], agr_s.at[p], zy_dev(p))
@@ -199,44 +224,49 @@
             total = total + fold(acc * acc) * valid
         norm[0] = total
 
-    norm_copy(0, core_dev).start()
+    def norm_out(j):
+        return rcopy(norm.at[0], normx.at[2 + zy], ns_s.at[2 + j], nr_s.at[2 + zy], zy_dev(peer(j)))
+
+    def norm_in(q):
+        return rcopy(norm.at[0], normx.at[2 + q], ns_s.at[2], nr_s.at[2 + q], zy_dev(q))
+
+    @pl.loop(1, zy_n)
+    def _(j):
+        norm_out(j).start()
+
+    @pl.when(zy < np_n)
+    def _():
+        @pl.loop(1, outer_n)
+        def _(j):
+            gather_copy(j).start()
+
+        inner_copy(zy).start()
+
+    normx[2 + zy] = norm[0]
+
+    @pl.loop(1, zy_n)
+    def _(j):
+        norm_in(peer(j)).wait_recv()
+
+    norm[1] = lax.fori_loop(0, zy_n, lambda q, acc: acc + normx[2 + q], jnp.zeros((8, 128), F32))
+    norm_first = rcopy(norm.at[1], normx.at[0], ns_s.at[0], nr_s.at[0], core_dev)
+    norm_first.start()
 
     @pl.when(zy < np_n)
     def _():
         forward(c, zy).start()
 
-        @pl.loop(1, zy_n)
-        def _(j):
-            gather_copy(j).start()
-
-    norm_copy(0, core_dev).wait_recv()
-    norm[1] = norm[0] + normx[0]
-    norm_copy(1, x_dev).start()
-    norm_copy(1, x_dev).wait_recv()
-    norm[2] = norm[1] + normx[1]
-
-    def norm_out(j):
-        return rcopy(norm.at[2], normx.at[2 + zy], ns_s.at[2 + j], nr_s.at[2 + zy], zy_dev(peer(j)))
-
-    def norm_in(s):
-        return rcopy(norm.at[2], normx.at[2 + s], ns_s.at[2], nr_s.at[2 + s], zy_dev(s))
-
-    @pl.loop(1, zy_n)
-    def _(j):
-        norm_out(j).start()
-
-    normx[2 + zy] = norm[2]
-
-    @pl.loop(1, zy_n)
-    def _(j):
-        norm_in(peer(j)).wait_recv()
-
-    total = lax.fori_loop(0, zy_n, lambda s, acc: acc + normx[2 + s], jnp.zeros((8, 128), F32))
+    norm_first.wait_recv()
+    norm[2] = norm[1] + normx[0]
+    norm_last = rcopy(norm.at[2], normx.at[1], ns_s.at[1], nr_s.at[1], x_dev)
+    norm_last.start()
+    norm_last.wait_recv()
+    total = norm[2] + normx[1]
     total = jnp.sum(jnp.sum(total, axis=1, keepdims=True), axis=0, keepdims=True)
     limit = jnp.sqrt(jnp.full((1, 1), D * D + D * KV, F32))
     clip = jnp.minimum(1.0, limit / (jnp.sqrt(total) + 1e-06))
 
-    for one in states_in:
+    for one in states_in[:3]:
         one.wait()
 
     def weights_over(p):
@@ -268,26 +298,41 @@
                 sk[row, :] = ks
                 w[x, core, p, tile(t), :] = join(m, km).astype(BF16)
 
-    outs = [(mq, nmq_hbm), (oq, noq_hbm), (sq, nsq_hbm), (mk, nmk_hbm), (ok, nok_hbm), (sk, nsk_hbm)]
-
     def out_copies(core, n):
         row = pl.ds(pl.multiple_of(core * rpc, RT), rpc)
         return [
             pltpu.make_async_copy(src.at[row, :], dst.at[row, :], out_sem.at[n, i])
-            for i, (src, dst) in enumerate(outs)
+            for i, (src, dst) in enumerate([(mq, nmq_hbm), (oq, noq_hbm), (sq, nsq_hbm)])
         ]
 
-    @pl.loop(0, np_n)
-    def _(k):
-        p = lax.rem(zy + np_n - k, np_n)
-
-        @pl.when(p != zy)
+    def use(p):
+        update(c, p)
+        weights_over(p).start()
+
+    @pl.when(zy < np_n)
+    def _():
+        use(zy)
+
+    @pl.loop(1, outer_n)
+    def _(j):
+        p = lax.rem(outer + outer_n - j, outer_n) * 2 + inner
+
+        @pl.when(p < np_n)
+        def _():
+            gather_arrival(p).wait_recv()
+            inner_copy(p).start()
+            forward(c, p).start()
+            use(p)
+
+    @pl.loop(0, outer_n)
+    def _(j):
+        p = lax.rem(outer + outer_n - j, outer_n) * 2 + 1 - inner
+
+        @pl.when(p < np_n)
         def _():
             gather_arrival(p).wait_recv()
             forward(c, p).start()
-
-        update(c, p)
-        weights_over(p).start()
+            use(p)
 
     mine_out = out_copies(c, 0)
     for one in mine_out:
@@ -302,6 +347,12 @@
     other_out = out_copies(1 - c, 1)
     for one in other_out:
         one.start()
+    keys_out = []
+    for i, (src, mid, dst) in enumerate([(mk, mkt, nmk_hbm), (ok, okt, nok_hbm), (sk, skt, nsk_hbm)]):
+        mid[...] = src[...].T
+        one = pltpu.make_async_copy(mid, dst, out_sem.at[0, 3 + i])
+        one.start()
+        keys_out.append(one)
     w_own = pltpu.make_async_copy(w.at[x], w_hbm.at[x], w_sem.at[0])
     w_own.start()
 
@@ -334,9 +385,13 @@
         weights_over(k).wait_send()
         weights_forward(k).wait_send()
 
+        @pl.when(lax.rem(k, 2) == inner)
+        def _():
+            inner_copy(k).wait_send()
+
     @pl.when(zy < np_n)
     def _():
-        @pl.loop(1, zy_n)
+        @pl.loop(1, outer_n)
         def _(j):
             gather_copy(j).wait_send()
 
@@ -344,9 +399,9 @@
     def _(j):
         norm_out(j).wait_send()
 
-    norm_copy(0, core_dev).wait_send()
-    norm_copy(1, x_dev).wait_send()
-    for one in mine_out + other_out + [w_own, w_c, w_o]:
+    norm_first.wait_send()
+    norm_last.wait_send()
+    for one in mine_out + other_out + keys_out + [w_own, w_c, w_o]:
         one.wait()
 
 
@@ -357,7 +412,9 @@
     per = -(-tiles_all // zy_n)
     np_n = -(-tiles_all // per)
     pr = per * RT
-    states = [master_query, moment_query, second_query, master_keys, moment_keys, second_keys]
+    keys = [master_keys, moment_keys, second_keys]
+    states = [master_query, moment_query, second_query] + [a.T for a in keys]
+    grads_keys = grads_keys.transpose(0, 2, 1)
     sem = lambda n: pltpu.SemaphoreType.DMA((n,))
     any_spec = pl.BlockSpec(memory_space=pl.ANY)
     outs = pl.pallas_call(
@@ -370,7 +427,8 @@
             pltpu.VMEM(grads_query.shape, BF16),
             pltpu.VMEM(grads_keys.shape, BF16),
         ]
-        + [pltpu.VMEM(a.shape, F32) for a in states]
+        + [pltpu.VMEM(a.shape, F32) for a in states + keys]
+        + [pltpu.VMEM((grads_keys.shape[2], grads_keys.shape[1]), F32)]
         + [
             pltpu.VMEM((np_n, 2, pr, WIDE), BF16),
             pltpu.VMEM((np_n, 2, pr, WIDE), BF16),
@@ -383,18 +441,18 @@
             pltpu.VMEM((2, CORES, np_n, pr, WIDE), BF16),
             pltpu.VMEM((3, 8, 128), F32),
             pltpu.VMEM((2 + zy_n, 8, 128), F32),
-            sem(2), sem(6), pltpu.SemaphoreType.DMA((2, 6)), sem(3),
+            sem(5), sem(6), pltpu.SemaphoreType.DMA((2, 6)), sem(3),
             sem(np_n), sem(np_n), sem(np_n), sem(np_n), sem(np_n), sem(zy_n),
-            sem(zy_n), sem(np_n), sem(np_n), sem(np_n),
+            sem(zy_n), sem(np_n), sem(np_n), sem(np_n), sem(np_n),
             sem(np_n), sem(np_n), sem(np_n), sem(np_n), sem(2 + zy_n), sem(2 + zy_n),
         ],
         compiler_params=pltpu.CompilerParams(
             collective_id=0, has_side_effects=True, vmem_limit_bytes=56 << 20
         ),
-    )(grads_query, master_query, moment_query, second_query, grads_keys, master_keys, moment_keys, second_keys)
+    )(grads_query, *states[:3], grads_keys, *states[3:])
     weights = outs[6].reshape(2, CORES, np_n * pr, WIDE)[:, :, :rpc, :].reshape(2 * half, WIDE)
     weight_query, weight_keys = split(weights)
-    return (*outs[0:3], weight_query, *outs[3:6], weight_keys)
+    return (*outs[0:3], weight_query, *[a.T for a in outs[3:6]], weight_keys)
 
 
 def solution(mesh):

time: 89.1 us -> 72.3 us (0.81)
  Pallas kernels: 65.7 us -> 57.3 us
  local copies, waits for them, and re-layouts: 22.2 us -> 13.9 us
    unnamed x25 -> x19, local copies, waits for them, and re-layouts: 20.4 us -> 10.4 us
    pallas_call x1, Pallas kernels: 65.7 us -> 57.3 us  [local(): pl.pallas_call(functools.partial(kernel, zy_n, np_n, pr, rpc), out_shape=...]
    slice x1, local copies, waits for them, and re-layouts: 0.16 us -> 1.86 us  [local(): outs[6].reshape(2, CORES, np_n * pr, WIDE)[:, :, :rpc, :]]
where the time goes in v2:
time: 72.3 us; the launch traced here: 72 us
  Pallas kernels  57.3 us (79%)
  local copies, waits for them, and re-layouts  13.9 us (19%)
    pallas_call x1, Pallas kernels, local(): pl.pallas_call(functools.partial(kernel, zy_n, np_n, pr, rpc), out_shape=...  57.3 us
    unnamed x19, local copies, waits for them, and re-layouts  10.4 us
    slice x1, local copies, waits for them, and re-layouts, local(): outs[6].reshape(2, CORES, np_n * pr, WIDE)[:, :, :rpc, :]  1.86 us
    slice x1, local copies, waits for them, and re-layouts, split(): wide[:, :D]  1.54 us

profile of v2, /device:TPU:1, one launch (start us, length us, event | category | flops | bytes accessed | tf_op | source)
XLA Modules:
  0.0 72.0 jit_solution(5619919173183963698)
XLA Ops:
  0.6 57.3 %shard_map.143 = (f32[480,960]{1,0:T(8,128)}, f32[480,960]{1,0:T(8,128)}, f32[480,960]{1,0:T(8,128)}, f32[320,480]{1,0:T(8,128)}, f32[320,480]{1,0:T(8,128)}, /*...) custom-call(bf16[2,960,960]{2,1,0:T(8,128)(2,1)} %gq_hbm.1, f32[480,960]{1,0:T(8,128)} %mq_hbm.1, ...), custom_call_target="tpu_custom_call" | custom-call | tf_op jit(solution)/shard_map/pallas_call | solution.py:420
  57.9 1.9 %slice.16 = bf16[2,2,240,1280]{3,2,1,0:T(8,128)(2,1)S(1)} slice(bf16[2,2,256,1280]{3,2,1,0:T(8,128)(2,1)} %bitcast.12), slice={[0:2], [0:2], [0:240], [0:1280]} | slice | bytes 4915200 | tf_op jit(solution)/shard_map/slice | solution.py:453
  59.8 0.1 slice.19
  60.0 0.1 pad_maximum_fusion
  60.1 1.1 %copy.18 = bf16[960,320]{0,1:T(8,128)(2,1)} copy(bf16[960,320]{1,0:T(8,128)(2,1)S(1)} %pad_maximum_fusion) | data formatting | bytes 1228800
  61.2 0.0 copy-start.2
  61.2 1.5 %slice.17 = bf16[960,960]{1,0:T(8,128)(2,1)} slice(bf16[960,1280]{1,0:T(8,128)(2,1)S(1)} %bitcast.11), slice={[0:960], [0:960]} | slice | bytes 3686400 | tf_op jit(solution)/shard_map/slice | solution.py:28
  62.7 0.7 copy-done.2
  63.4 0.0 copy-start.1
  63.4 1.3 %copy.25 = f32[480,960]{1,0:T(8,128)} copy(f32[480,960]{1,0:T(8,128)S(1)} %copy-done.2) | data formatting | bytes 3686400
  64.7 1.0 %copy-done.1 = f32[480,960]{1,0:T(8,128)S(1)} copy-done((f32[480,960]{1,0:T(8,128)S(1)}, f32[480,960]{1,0:T(8,128)}, u32[]{:S(2)}) %copy-start.1) | copy-done | bytes 1843224
  65.7 0.0 copy-start
  65.7 1.3 %copy.26 = f32[480,960]{1,0:T(8,128)} copy(f32[480,960]{1,0:T(8,128)S(1)} %copy-done.1) | data formatting | bytes 3686400
  66.9 1.0 %copy-done = f32[480,960]{1,0:T(8,128)S(1)} copy-done((f32[480,960]{1,0:T(8,128)S(1)}, f32[480,960]{1,0:T(8,128)}, u32[]{:S(2)}) %copy-start) | copy-done | bytes 1843224
  67.9 0.0 copy-start.5
  67.9 0.0 copy-start.4
  67.9 1.3 %copy.27 = f32[480,960]{1,0:T(8,128)} copy(f32[480,960]{1,0:T(8,128)S(1)} %copy-done) | data formatting | bytes 3686400
  69.2 0.3 copy-done.5
  69.5 0.0 copy-start.3
  69.5 0.8 %copy.28 = f32[480,320]{0,1:T(8,128)} copy(f32[480,320]{0,1:T(8,128)S(1)} %bitcast.19) | data formatting | bytes 1228800
  70.3 0.0 copy-done.4
  70.3 0.8 %copy.29 = f32[480,320]{0,1:T(8,128)} copy(f32[480,320]{0,1:T(8,128)S(1)} %bitcast.18) | data formatting | bytes 1228800
  71.1 0.0 copy-done.3
  71.1 0.8 %copy.30 = f32[480,320]{0,1:T(8,128)} copy(f32[480,320]{0,1:T(8,128)S(1)} %bitcast.17) | data formatting | bytes 1228800
  (1 shorter events, 0.0 us)
Async XLA Ops:
  61.2 2.3 %copy-start.2 = (f32[480,960]{1,0:T(8,128)S(1)}, f32[480,960]{1,0:T(8,128)}, u32[]{:S(2)}) copy-start(f32[480,960]{1,0:T(8,128)} %get-tuple-element.46) | copy-start | bytes 5529604
  63.4 2.3 %copy-start.1 = (f32[480,960]{1,0:T(8,128)S(1)}, f32[480,960]{1,0:T(8,128)}, u32[]{:S(2)}) copy-start(f32[480,960]{1,0:T(8,128)} %get-tuple-element.47) | copy-start | bytes 5529604
  65.7 2.3 %copy-start = (f32[480,960]{1,0:T(8,128)S(1)}, f32[480,960]{1,0:T(8,128)}, u32[]{:S(2)}) copy-start(f32[480,960]{1,0:T(8,128)} %get-tuple-element.48) | copy-start | bytes 5529604
  67.9 1.5 %copy-start.5 = (f32[320,480]{1,0:T(8,128)S(1)}, f32[320,480]{1,0:T(8,128)}, u32[]{:S(2)}) copy-start(f32[320,480]{1,0:T(8,128)} %get-tuple-element.19) | copy-start | bytes 1843204
  67.9 2.4 %copy-start.4 = (f32[320,480]{1,0:T(8,128)S(1)}, f32[320,480]{1,0:T(8,128)}, u32[]{:S(2)}) copy-start(f32[320,480]{1,0:T(8,128)} %get-tuple-element.20) | copy-start | bytes 1843204
  69.5 1.7 %copy-start.3 = (f32[320,480]{1,0:T(8,128)S(1)}, f32[320,480]{1,0:T(8,128)}, u32[]{:S(2)}) copy-start(f32[320,480]{1,0:T(8,128)} %get-tuple-element.21) | copy-start | bytes 1843204

commit v3 on v2

--- a/solution.py
+++ b/solution.py
@@ -32,8 +32,8 @@
     grad = clip * grad_sum
     new_moment = 0.9 * moment + 0.1 * grad
     new_second = 0.999 * second + 0.001 * grad * grad
-    mhat = new_moment / (1.0 - 0.9**STEP)
-    vhat = new_second / (1.0 - 0.999**STEP)
+    mhat = new_moment * (1.0 / (1.0 - 0.9**STEP))
+    vhat = new_second * (1.0 / (1.0 - 0.999**STEP))
     new_master = master - 0.02 * (mhat / (jnp.sqrt(vhat) + 1e-08) + 0.1 * master)
     return new_master, new_moment, new_second
 
@@ -41,12 +41,12 @@
 def kernel(
     zy_n, np_n, pr, rpc,
     gq_hbm, mq_hbm, oq_hbm, sq_hbm, gk_hbm, mk_hbm, ok_hbm, sk_hbm,
-    nmq_hbm, noq_hbm, nsq_hbm, nmk_hbm, nok_hbm, nsk_hbm, w_hbm,
+    g_hbm, w_hbm, clip_ref,
     gq, gk, mq, oq, sq, mkt, okt, skt, mk, ok, sk, lk,
     cs, cr, xs, xr, zs, zr, own, g, w, norm, normx,
-    in_sem, st_sem, out_sem, w_sem,
+    in_sem, st_sem, w_sem,
     cs_s, cr_s, xs_s, xr_s, zs_s, zr_s,
-    ags_s, agr_s, is_s, fs_s, fr_s, ws_s, wr_s, vs_s, vr_s, ns_s, nr_s,
+    ags_s, agr_s, is_s, fs_s, fr_s, ws_s, wr_s, vs_s, vr_s, us_s, ur_s, ns_s, nr_s,
 ):
     rep = lax.axis_index("rep")
     x = lax.axis_index("shard")
@@ -90,8 +90,10 @@
     for one in grads_in:
         one.start()
     states = [(mq_hbm, mq), (oq_hbm, oq), (sq_hbm, sq), (mk_hbm, mkt), (ok_hbm, okt), (sk_hbm, skt)]
+    mine = pl.ds(pl.multiple_of(c * rpc, RT), rpc)
     states_in = [
-        pltpu.make_async_copy(src, dst, st_sem.at[i]) for i, (src, dst) in enumerate(states)
+        pltpu.make_async_copy(src.at[mine, :] if i < 3 else src, dst, st_sem.at[i])
+        for i, (src, dst) in enumerate(states)
     ]
 
     barrier = pltpu.get_barrier_semaphore()
@@ -266,6 +268,7 @@
     limit = jnp.sqrt(jnp.full((1, 1), D * D + D * KV, F32))
     clip = jnp.minimum(1.0, limit / (jnp.sqrt(total) + 1e-06))
 
+    clip_ref[...] = jnp.broadcast_to(clip, (8, 128))
     for one in states_in[:3]:
         one.wait()
 
@@ -281,33 +284,22 @@
     def weights_last(p):
         return rcopy(w.at[1 - x, 1 - c, p], w.at[1 - x, 1 - c, p], vs_s.at[p], vr_s.at[p], core_dev)
 
-    def update(core, p):
+    def weights_near(p):
+        return rcopy(w.at[x, c, p], w.at[x, c, p], us_s.at[p], ur_s.at[p], core_dev)
+
+    def weights_near_in(p):
+        return rcopy(w.at[x, 1 - c, p], w.at[x, 1 - c, p], us_s.at[p], ur_s.at[p], core_dev)
+
+    def use(p):
         for t in range(tiles):
-            row = pl.ds(pl.multiple_of(core * rpc + rows_of(p, t), RT), RT)
-
-            @pl.when(p * pr + t * RT < rpc)
-            def _():
-                gsq, gsk = split(g[core, p, tile(t), :].astype(F32))
-                m, o, s = adamw(gsq, mq[row, :], oq[row, :], sq[row, :], clip)
-                mq[row, :] = m
-                oq[row, :] = o
-                sq[row, :] = s
-                km, ko, ks = adamw(gsk, mk[row, :], ok[row, :], sk[row, :], clip)
-                mk[row, :] = km
-                ok[row, :] = ko
-                sk[row, :] = ks
-                w[x, core, p, tile(t), :] = join(m, km).astype(BF16)
-
-    def out_copies(core, n):
-        row = pl.ds(pl.multiple_of(core * rpc, RT), rpc)
-        return [
-            pltpu.make_async_copy(src.at[row, :], dst.at[row, :], out_sem.at[n, i])
-            for i, (src, dst) in enumerate([(mq, nmq_hbm), (oq, noq_hbm), (sq, nsq_hbm)])
-        ]
-
-    def use(p):
-        update(c, p)
+            row = pl.ds(pl.multiple_of(rows_of(p, t), RT), RT)
+            key_row = pl.ds(pl.multiple_of(c * rpc + rows_of(p, t), RT), RT)
+            gsq, gsk = split(g[c, p, tile(t), :].astype(F32))
+            new_q = adamw(gsq, mq[row, :], oq[row, :], sq[row, :], clip)[0]
+            new_k = adamw(gsk, mk[key_row, :], ok[key_row, :], sk[key_row, :], clip)[0]
+            w[x, c, p, tile(t), :] = join(new_q, new_k).astype(BF16)
         weights_over(p).start()
+        weights_near(p).start()
 
     @pl.when(zy < np_n)
     def _():
@@ -334,27 +326,22 @@
             forward(c, p).start()
             use(p)
 
-    mine_out = out_copies(c, 0)
-    for one in mine_out:
-        one.start()
-
-    @pl.loop(0, np_n)
-    def _(k):
-        p = lax.rem(zy + np_n - k, np_n)
+    w_own = pltpu.make_async_copy(w.at[x, c], w_hbm.at[x, c], w_sem.at[0])
+    w_own.start()
+
+    @pl.loop(0, np_n)
+    def _(p):
         forward(1 - c, p).wait_recv()
-        update(1 - c, p)
-
-    other_out = out_copies(1 - c, 1)
-    for one in other_out:
-        one.start()
-    keys_out = []
-    for i, (src, mid, dst) in enumerate([(mk, mkt, nmk_hbm), (ok, okt, nok_hbm), (sk, skt, nsk_hbm)]):
-        mid[...] = src[...].T
-        one = pltpu.make_async_copy(mid, dst, out_sem.at[0, 3 + i])
-        one.start()
-        keys_out.append(one)
-    w_own = pltpu.make_async_copy(w.at[x], w_hbm.at[x], w_sem.at[0])
-    w_own.start()
+
+    g_out = pltpu.make_async_copy(g, g_hbm, w_sem.at[3])
+    g_out.start()
+
+    @pl.loop(0, np_n)
+    def _(p):
+        weights_near_in(p).wait_recv()
+
+    w_near = pltpu.make_async_copy(w.at[x, 1 - c], w_hbm.at[x, 1 - c], w_sem.at[4])
+    w_near.start()
 
     @pl.loop(0, np_n)
     def _(k):
@@ -384,6 +371,7 @@
         forward(c, k).wait_send()
         weights_over(k).wait_send()
         weights_forward(k).wait_send()
+        weights_near(k).wait_send()
 
         @pl.when(lax.rem(k, 2) == inner)
         def _():
@@ -401,7 +389,120 @@
 
     norm_first.wait_send()
     norm_last.wait_send()
-    for one in mine_out + other_out + keys_out + [w_own, w_c, w_o]:
+    for one in [w_own, w_near, g_out, w_c, w_o]:
+        one.wait()
+
+
+def finish(
+    np_n, pr, rpc,
+    mq_hbm, oq_hbm, sq_hbm, mk_hbm, ok_hbm, sk_hbm, g_hbm, w_hbm, clip_ref,
+    nmq_hbm, noq_hbm, nsq_hbm, nmk_hbm, nok_hbm, nsk_hbm, wq_hbm, wk_hbm,
+    mq, oq, sq, mk, ok, sk, g, w, wq, wk, wk_rows, gk_rows, gk,
+    in_sem, out_sem, more_sem, end_sem,
+):
+    tiles_all = rpc // RT
+    tiles = pr // RT
+    parts = 3 if tiles_all % 3 == 0 else 1
+    step = tiles_all // parts
+    half = CORES * rpc
+    clip = clip_ref[0:1, 0:1]
+
+    def block(n):
+        return slice(n * step * RT, (n + 1) * step * RT)
+
+    def q_in(n):
+        return [
+            pltpu.make_async_copy(src.at[block(n), :], dst.at[block(n), :], in_sem.at[n, i])
+            for i, (src, dst) in enumerate([(mq_hbm, mq), (oq_hbm, oq), (sq_hbm, sq)])
+        ]
+
+    def q_out(n):
+        return [
+            pltpu.make_async_copy(src.at[block(n), :], dst.at[block(n), :], out_sem.at[n, i])
+            for i, (src, dst) in enumerate([(mq, nmq_hbm), (oq, noq_hbm), (sq, nsq_hbm)])
+        ]
+
+    g_in = [pltpu.make_async_copy(g_hbm.at[a], g.at[a], more_sem.at[a]) for a in range(CORES)]
+    w_in = [pltpu.make_async_copy(w_hbm.at[a], w.at[a], more_sem.at[CORES + a]) for a in range(2)]
+    k_in = [
+        pltpu.make_async_copy(src, dst, more_sem.at[CORES + 2 + i])
+        for i, (src, dst) in enumerate([(mk_hbm, mk), (ok_hbm, ok), (sk_hbm, sk)])
+    ]
+    total = CORES * parts
+    w_in[0].start()
+    g_in[0].start()
+    for n in range(total):
+        for one in q_in(n):
+            one.start()
+        if n == 0:
+            for one in w_in[1:] + g_in[1:]:
+                one.start()
+    for one in k_in:
+        one.start()
+    ends = []
+
+    def end(i, src, dst):
+        one = pltpu.make_async_copy(src, dst, end_sem.at[i])
+        one.start()
+        ends.append(one)
+
+    def weights(xh):
+        w_in[xh].wait()
+        for core in range(CORES):
+
+            @pl.loop(0, tiles_all)
+            def _(i):
+                row = pl.ds(pl.multiple_of(xh * half + core * rpc + i * RT, RT), RT)
+                at = pl.ds(pl.multiple_of(lax.rem(i, tiles) * RT, RT), RT)
+                q, k = split(w[xh, core, lax.div(i, tiles), at, :].astype(F32))
+                wq[row, :] = q.astype(BF16)
+                wk_rows[row, :] = k
+
+        both = slice(xh * half, (xh + 1) * half)
+        end(xh, wq.at[both, :], wq_hbm.at[both, :])
+
+    def update(n):
+        core = n // parts
+        if n % parts == 0:
+            g_in[core].wait()
+        for one in q_in(n):
+            one.wait()
+
+        @pl.loop(n % parts * step, (n % parts + 1) * step)
+        def _(i):
+            row = pl.ds(pl.multiple_of(core * rpc + i * RT, RT), RT)
+            at = pl.ds(pl.multiple_of(lax.rem(i, tiles) * RT, RT), RT)
+            gsq, gsk = split(g[core, lax.div(i, tiles), at, :].astype(F32))
+            mq[row, :], oq[row, :], sq[row, :] = adamw(gsq, mq[row, :], oq[row, :], sq[row, :], clip)
+            gk_rows[row, :] = gsk
+
+        for one in q_out(n):
+            one.start()
+
+    weights(0)
+    update(0)
+    weights(1)
+    for n in range(1, total):
+        update(n)
+    for lane in range(0, wk.shape[1], 128):
+        lanes = slice(lane, min(lane + 128, wk.shape[1]))
+        wk[:, lanes] = wk_rows[lanes, :].T.astype(BF16)
+    end(2, wk, wk_hbm)
+    gk[...] = gk_rows[...].T
+    for one in k_in:
+        one.wait()
+
+    @pl.loop(0, gk.shape[0] // RT)
+    def _(i):
+        row = pl.ds(pl.multiple_of(i * RT, RT), RT)
+        mk[row, :], ok[row, :], sk[row, :] = adamw(gk[row, :], mk[row, :], ok[row, :], sk[row, :], clip)
+
+    for i, (src, dst) in enumerate([(mk, nmk_hbm), (ok, nok_hbm), (sk, nsk_hbm)]):
+        end(3 + i, src, dst)
+    for n in range(total):
+        for one in q_out(n):
+            one.wait()
+    for one in ends:
         one.wait()
 
 
@@ -417,17 +518,21 @@
     grads_keys = grads_keys.transpose(0, 2, 1)
     sem = lambda n: pltpu.SemaphoreType.DMA((n,))
     any_spec = pl.BlockSpec(memory_space=pl.ANY)
-    outs = pl.pallas_call(
+    sums, weights, clip = pl.pallas_call(
         functools.partial(kernel, zy_n, np_n, pr, rpc),
-        out_shape=[jax.ShapeDtypeStruct(a.shape, F32) for a in states]
-        + [jax.ShapeDtypeStruct((2, CORES, np_n, pr, WIDE), BF16)],
+        out_shape=[
+            jax.ShapeDtypeStruct((CORES, np_n, pr, WIDE), BF16),
+            jax.ShapeDtypeStruct((2, CORES, np_n, pr, WIDE), BF16),
+            jax.ShapeDtypeStruct((8, 128), F32),
+        ],
         in_specs=[any_spec] * 8,
-        out_specs=[any_spec] * 7,
+        out_specs=[any_spec, any_spec, pl.BlockSpec(memory_space=pltpu.VMEM)],
         scratch_shapes=[
             pltpu.VMEM(grads_query.shape, BF16),
             pltpu.VMEM(grads_keys.shape, BF16),
         ]
-        + [pltpu.VMEM(a.shape, F32) for a in states + keys]
+        + [pltpu.VMEM((rpc, D), F32)] * 3
+        + [pltpu.VMEM(a.shape, F32) for a in states[3:] + keys]
         + [pltpu.VMEM((grads_keys.shape[2], grads_keys.shape[1]), F32)]
         + [
             pltpu.VMEM((np_n, 2, pr, WIDE), BF16),
@@ -441,18 +546,38 @@
             pltpu.VMEM((2, CORES, np_n, pr, WIDE), BF16),
             pltpu.VMEM((3, 8, 128), F32),
             pltpu.VMEM((2 + zy_n, 8, 128), F32),
-            sem(5), sem(6), pltpu.SemaphoreType.DMA((2, 6)), sem(3),
+            sem(5), sem(6), sem(5),
             sem(np_n), sem(np_n), sem(np_n), sem(np_n), sem(np_n), sem(zy_n),
             sem(zy_n), sem(np_n), sem(np_n), sem(np_n), sem(np_n),
-            sem(np_n), sem(np_n), sem(np_n), sem(np_n), sem(2 + zy_n), sem(2 + zy_n),
+            sem(np_n), sem(np_n), sem(np_n), sem(np_n), sem(np_n), sem(np_n), sem(2 + zy_n), sem(2 + zy_n),
         ],
         compiler_params=pltpu.CompilerParams(
             collective_id=0, has_side_effects=True, vmem_limit_bytes=56 << 20
         ),
     )(grads_query, *states[:3], grads_keys, *states[3:])
-    weights = outs[6].reshape(2, CORES, np_n * pr, WIDE)[:, :, :rpc, :].reshape(2 * half, WIDE)
-    weight_query, weight_keys = split(weights)
-    return (*outs[0:3], weight_query, *[a.T for a in outs[3:6]], weight_keys)
+    parts = 3 if tiles_all % 3 == 0 else 1
+    outs = pl.pallas_call(
+        functools.partial(finish, np_n, pr, rpc),
+        out_shape=[jax.ShapeDtypeStruct(a.shape, F32) for a in states]
+        + [jax.ShapeDtypeStruct((2 * half, D), BF16), jax.ShapeDtypeStruct((KV, 2 * half), BF16)],
+        in_specs=[any_spec] * 8 + [pl.BlockSpec(memory_space=pltpu.VMEM)],
+        out_specs=[any_spec] * 8,
+        scratch_shapes=[pltpu.VMEM(a.shape, F32) for a in states]
+        + [
+            pltpu.VMEM(sums.shape, BF16),
+            pltpu.VMEM(weights.shape, BF16),
+            pltpu.VMEM((2 * half, D), BF16),
+            pltpu.VMEM((KV, 2 * half), BF16),
+            pltpu.VMEM((2 * half, KV), F32),
+            pltpu.VMEM((half, KV), F32),
+            pltpu.VMEM((KV, half), F32),
+            pltpu.SemaphoreType.DMA((CORES * parts, 3)),
+            pltpu.SemaphoreType.DMA((CORES * parts, 3)),
+            sem(CORES + 5), sem(6),
+        ],
+        compiler_params=pltpu.CompilerParams(vmem_limit_bytes=56 << 20),
+    )(*states, sums, weights, clip)
+    return (*outs[:3], outs[6], *[a.T for a in outs[3:6]], outs[7].T)
 
 
 def solution(mesh):

time: 72.3 us -> 71.6 us (level)
  local copies, waits for them, and re-layouts: 13.9 us -> 0 us
  Pallas kernels: 57.3 us -> 70.8 us
    pallas_call x0 -> x1, Pallas kernels: none -> 13 us  [local(): pl.pallas_call(functools.partial(finish, np_n, pr, rpc), out_shape=[jax.S...]
    unnamed x19 -> x0, local copies, waits for them, and re-layouts: 10.4 us -> none
    slice x4 -> x0, local copies, waits for them, and re-layouts: 3.56 us -> none  [the longest x1 1.86 us: local(): outs[6].reshape(2, CORES, np_n * pr, WIDE)[:, :, :rpc, :]]
where the time goes in v3:
time: 71.6 us; the launch traced here: 71.5 us
  Pallas kernels  70.8 us (99%)
    pallas_call x1, Pallas kernels, local(): pl.pallas_call(functools.partial(kernel, zy_n, np_n, pr, rpc), out_shape=...  57.9 us
    pallas_call x1, Pallas kernels, local(): pl.pallas_call(functools.partial(finish, np_n, pr, rpc), out_shape=[jax.S...  13 us

profile of v3, /device:TPU:1, one launch (start us, length us, event | category | flops | bytes accessed | tf_op | source)
XLA Modules:
  0.0 71.5 jit_solution(10075523973247678275)
XLA Ops:
  0.6 57.9 %shard_map.143 = (bf16[2,8,32,1280]{3,2,1,0:T(8,128)(2,1)}, bf16[2,2,8,32,1280]{4,3,2,1,0:T(8,128)(2,1)}, f32[8,128]{1,0:T(8,128)}) custom-call(bf16[2,960,960]{2,1,0:T(8,128)(2,1)} %gq_hbm.1, f32[480,960]{1,0:T(8,128)} %mq_hbm.3, f32[480,960]{1,0:T(8,128)} %oq_hbm.3, f32[480,960]{1,0:T(8,128)} %sq_hbm.3, bf16[2,320,960]{2,1,0:T(8,128)(2,1)} %bitcast.14, ...), custom_call_target="tpu_custom_call" | custom-call | tf_op jit(solution)/shard_map/pallas_call | solution.py:521
  58.5 13.0 %shard_map.144 = (f32[480,960]{1,0:T(8,128)}, f32[480,960]{1,0:T(8,128)}, f32[480,960]{1,0:T(8,128)}, f32[320,480]{1,0:T(8,128)}, f32[320,480]{1,0:T(8,128)}, /*...) custom-call(f32[480,960]{1,0:T(8,128)} %mq_hbm.3, f32[480,960]{1,0:T(8,128)} %oq_hbm.3, ...), custom_call_target="tpu_custom_call" | custom-call | tf_op jit(solution)/shard_map/pallas_call | solution.py:559

commit v4 on v3

--- a/solution.py
+++ b/solution.py
@@ -46,7 +46,7 @@
     cs, cr, xs, xr, zs, zr, own, g, w, norm, normx,
     in_sem, st_sem, w_sem,
     cs_s, cr_s, xs_s, xr_s, zs_s, zr_s,
-    ags_s, agr_s, is_s, fs_s, fr_s, ws_s, wr_s, vs_s, vr_s, us_s, ur_s, ns_s, nr_s,
+    ags_s, agr_s, is_s, fs_s, fr_s, ws_s, wr_s, ys_s, vs_s, vr_s, us_s, ur_s, ns_s, nr_s,
 ):
     rep = lax.axis_index("rep")
     x = lax.axis_index("shard")
@@ -278,6 +278,9 @@
     def weights_in(p):
         return rcopy(w.at[1 - x, c, p], w.at[1 - x, c, p], ws_s.at[p], wr_s.at[p], x_dev)
 
+    def weights_inner(p):
+        return rcopy(w.at[1 - x, c, p], w.at[1 - x, c, p], ys_s.at[p], wr_s.at[p], zy_dev(zy + 1 - 2 * inner))
+
     def weights_forward(p):
         return rcopy(w.at[1 - x, c, p], w.at[1 - x, c, p], vs_s.at[p], vr_s.at[p], core_dev)
 
@@ -298,12 +301,12 @@
             new_q = adamw(gsq, mq[row, :], oq[row, :], sq[row, :], clip)[0]
             new_k = adamw(gsk, mk[key_row, :], ok[key_row, :], sk[key_row, :], clip)[0]
             w[x, c, p, tile(t), :] = join(new_q, new_k).astype(BF16)
-        weights_over(p).start()
         weights_near(p).start()
 
     @pl.when(zy < np_n)
     def _():
         use(zy)
+        weights_over(zy).start()
 
     @pl.loop(1, outer_n)
     def _(j):
@@ -315,6 +318,17 @@
             inner_copy(p).start()
             forward(c, p).start()
             use(p)
+            weights_over(p).start()
+
+    @pl.loop(0, outer_n)
+    def _(j):
+        p = lax.rem(outer + outer_n - j, outer_n) * 2 + inner
+
+        @pl.when(p < np_n)
+        def _():
+            weights_in(p).wait_recv()
+            weights_inner(p).start()
+            weights_forward(p).start()
 
     @pl.loop(0, outer_n)
     def _(j):
@@ -343,11 +357,14 @@
     w_near = pltpu.make_async_copy(w.at[x, 1 - c], w_hbm.at[x, 1 - c], w_sem.at[4])
     w_near.start()
 
-    @pl.loop(0, np_n)
-    def _(k):
-        p = lax.rem(zy + np_n - k, np_n)
-        weights_in(p).wait_recv()
-        weights_forward(p).start()
+    @pl.loop(0, outer_n)
+    def _(j):
+        p = lax.rem(outer + outer_n - j, outer_n) * 2 + 1 - inner
+
+        @pl.when(p < np_n)
+        def _():
+            weights_in(p).wait_recv()
+            weights_forward(p).start()
 
     w_c = pltpu.make_async_copy(w.at[1 - x, c], w_hbm.at[1 - x, c], w_sem.at[1])
     w_c.start()
@@ -369,13 +386,14 @@
             zy_copy(k).wait_send()
 
         forward(c, k).wait_send()
-        weights_over(k).wait_send()
         weights_forward(k).wait_send()
         weights_near(k).wait_send()
 
         @pl.when(lax.rem(k, 2) == inner)
         def _():
             inner_copy(k).wait_send()
+            weights_over(k).wait_send()
+            weights_inner(k).wait_send()
 
     @pl.when(zy < np_n)
     def _():
@@ -482,12 +500,12 @@
     weights(0)
     update(0)
     weights(1)
-    for n in range(1, total):
-        update(n)
     for lane in range(0, wk.shape[1], 128):
         lanes = slice(lane, min(lane + 128, wk.shape[1]))
         wk[:, lanes] = wk_rows[lanes, :].T.astype(BF16)
     end(2, wk, wk_hbm)
+    for n in range(1, total):
+        update(n)
     gk[...] = gk_rows[...].T
     for one in k_in:
         one.wait()
@@ -549,7 +567,7 @@
             sem(5), sem(6), sem(5),
             sem(np_n), sem(np_n), sem(np_n), sem(np_n), sem(np_n), sem(zy_n),
             sem(zy_n), sem(np_n), sem(np_n), sem(np_n), sem(np_n),
-            sem(np_n), sem(np_n), sem(np_n), sem(np_n), sem(np_n), sem(np_n), sem(2 + zy_n), sem(2 + zy_n),
+            sem(np_n), sem(np_n), sem(np_n), sem(np_n), sem(np_n), sem(np_n), sem(np_n), sem(2 + zy_n), sem(2 + zy_n),
         ],
         compiler_params=pltpu.CompilerParams(
             collective_id=0, has_side_effects=True, vmem_limit_bytes=56 << 20

time: 71.6 us -> 69 us (0.964)
  Pallas kernels: 70.8 us -> 68.1 us
    pallas_call x1, Pallas kernels: 57.9 us -> 55.1 us  [local(): pl.pallas_call(functools.partial(kernel, zy_n, np_n, pr, rpc), out_shape=...]
where the time goes in v4:
time: 69 us; the launch traced here: 68.8 us
  Pallas kernels  68.1 us (99%)
    pallas_call x1, Pallas kernels, local(): pl.pallas_call(functools.partial(kernel, zy_n, np_n, pr, rpc), out_shape=...  55.1 us
    pallas_call x1, Pallas kernels, local(): pl.pallas_call(functools.partial(finish, np_n, pr, rpc), out_shape=[jax.S...  13 us

profile of v4, /device:TPU:1, one launch (start us, length us, event | category | flops | bytes accessed | tf_op | source)
XLA Modules:
  0.0 68.8 jit_solution(4270848622796819797)
XLA Ops:
  0.6 55.1 %shard_map.143 = (bf16[2,8,32,1280]{3,2,1,0:T(8,128)(2,1)}, bf16[2,2,8,32,1280]{4,3,2,1,0:T(8,128)(2,1)}, f32[8,128]{1,0:T(8,128)}) custom-call(bf16[2,960,960]{2,1,0:T(8,128)(2,1)} %gq_hbm.1, f32[480,960]{1,0:T(8,128)} %mq_hbm.3, f32[480,960]{1,0:T(8,128)} %oq_hbm.3, f32[480,960]{1,0:T(8,128)} %sq_hbm.3, bf16[2,320,960]{2,1,0:T(8,128)(2,1)} %bitcast.14, ...), custom_call_target="tpu_custom_call" | custom-call | tf_op jit(solution)/shard_map/pallas_call | solution.py:539
  55.7 13.0 %shard_map.144 = (f32[480,960]{1,0:T(8,128)}, f32[480,960]{1,0:T(8,128)}, f32[480,960]{1,0:T(8,128)}, f32[320,480]{1,0:T(8,128)}, f32[320,480]{1,0:T(8,128)}, /*...) custom-call(f32[480,960]{1,0:T(8,128)} %mq_hbm.3, f32[480,960]{1,0:T(8,128)} %oq_hbm.3, ...), custom_call_target="tpu_custom_call" | custom-call | tf_op jit(solution)/shard_map/pallas_call | solution.py:577

commit v5 on v4

--- a/solution.py
+++ b/solution.py
@@ -468,7 +468,7 @@
         w_in[xh].wait()
         for core in range(CORES):
 
-            @pl.loop(0, tiles_all)
+            @pl.loop(0, tiles_all, unroll=True)
             def _(i):
                 row = pl.ds(pl.multiple_of(xh * half + core * rpc + i * RT, RT), RT)
                 at = pl.ds(pl.multiple_of(lax.rem(i, tiles) * RT, RT), RT)
@@ -486,7 +486,7 @@
         for one in q_in(n):
             one.wait()
 
-        @pl.loop(n % parts * step, (n % parts + 1) * step)
+        @pl.loop(n % parts * step, (n % parts + 1) * step, unroll=True)
         def _(i):
             row = pl.ds(pl.multiple_of(core * rpc + i * RT, RT), RT)
             at = pl.ds(pl.multiple_of(lax.rem(i, tiles) * RT, RT), RT)
@@ -510,7 +510,7 @@
     for one in k_in:
         one.wait()
 
-    @pl.loop(0, gk.shape[0] // RT)
+    @pl.loop(0, gk.shape[0] // RT, unroll=4)
     def _(i):
         row = pl.ds(pl.multiple_of(i * RT, RT), RT)
         mk[row, :], ok[row, :], sk[row, :] = adamw(gk[row, :], mk[row, :], ok[row, :], sk[row, :], clip)

time: 69 us -> 65.4 us (0.948)
  Pallas kernels: 68.1 us -> 64.6 us
    pallas_call x1, Pallas kernels: 13 us -> 9.52 us  [local(): pl.pallas_call(functools.partial(finish, np_n, pr, rpc), out_shape=[jax.S...]
where the time goes in v5:
time: 65.4 us; the launch traced here: 65.3 us
  Pallas kernels  64.6 us (99%)
    pallas_call x1, Pallas kernels, local(): pl.pallas_call(functools.partial(kernel, zy_n, np_n, pr, rpc), out_shape=...  55.1 us
    pallas_call x1, Pallas kernels, local(): pl.pallas_call(functools.partial(finish, np_n, pr, rpc), out_shape=[jax.S...  9.52 us

profile of v5, /device:TPU:1, one launch (start us, length us, event | category | flops | bytes accessed | tf_op | source)
XLA Modules:
  0.0 65.3 jit_solution(4811166847585401288)
XLA Ops:
  0.6 55.1 %shard_map.143 = (bf16[2,8,32,1280]{3,2,1,0:T(8,128)(2,1)}, bf16[2,2,8,32,1280]{4,3,2,1,0:T(8,128)(2,1)}, f32[8,128]{1,0:T(8,128)}) custom-call(bf16[2,960,960]{2,1,0:T(8,128)(2,1)} %gq_hbm.1, f32[480,960]{1,0:T(8,128)} %mq_hbm.3, f32[480,960]{1,0:T(8,128)} %oq_hbm.3, f32[480,960]{1,0:T(8,128)} %sq_hbm.3, bf16[2,320,960]{2,1,0:T(8,128)(2,1)} %bitcast.14, ...), custom_call_target="tpu_custom_call" | custom-call | tf_op jit(solution)/shard_map/pallas_call | solution.py:539
  55.7 9.5 %shard_map.144 = (f32[480,960]{1,0:T(8,128)}, f32[480,960]{1,0:T(8,128)}, f32[480,960]{1,0:T(8,128)}, f32[320,480]{1,0:T(8,128)}, f32[320,480]{1,0:T(8,128)}, /*...) custom-call(f32[480,960]{1,0:T(8,128)} %mq_hbm.3, f32[480,960]{1,0:T(8,128)} %oq_hbm.3, ...), custom_call_target="tpu_custom_call" | custom-call | tf_op jit(solution)/shard_map/pallas_call | solution.py:577
